TPU v7x, 1024 devices: a whole 4x4x32 slice. The times are simulated.
1024 devices in a mesh: order: 32 (over x, z_lo), level: 32 (over z_hi, y, core).
Axes of the slice: x: 4, y: 4, z: 32 (z_hi: 4, z_lo: 8; z = z_hi * 8 + z_lo), core: 2. Of those that a mesh axis runs over, the one named last changes fastest.
Arguments:
- spectral: bfloat16 [512, 512, 2, 2, 128], P('order', 'level'), may hold values from -6 to 6
- factors: bfloat16 [512, 128, 128], P('level'), may hold values from -2 to 2
- legendre: bfloat16 [512, 512, 256], P('order'), may hold values from -12 to 12
- sigma: bfloat16 [256, 128, 1536], P('order', 'level'), may hold values from 0.5 to 2
- order_table: int32 [512], replicated, may hold values from 0 to 511, as said below
- degree_table: int32 [512], replicated, may hold values from 0 to 511, as said below
Outputs:
- grid: bfloat16 [256, 2, 128, 1536], P('order', None, 'level')
Inputs may be any that keep to these rules, and one draw needn't show every extreme that they name: `order_table`: a permutation of 0 to 511. `degree_table`: a permutation of 0 to 511.
All inputs are finite; a program needn't handle non-finite values.
Results may differ from a plain program's by a relative error of at most 0.0062.
Values may be sent and summed in bfloat16 or wider, within the bound.
No kernel may reach another device: no remote copies, remote signals or barrier semaphores. Data moves between devices by JAX's collectives and lax.ppermute only.
A program may use at most 32 MiB of HBM per device.

v0:
```python
import jax
import jax.numpy as jnp
from jax import lax
from jax.sharding import PartitionSpec as P


def per_device(spectral, factors, legendre, sigma, order_table, degree_table):
    local_orders = spectral.shape[0]
    local_degrees = spectral.shape[1]
    points = sigma.shape[2]
    my_orders = lax.dynamic_slice_in_dim(
        order_table, lax.axis_index("order") * local_orders, local_orders
    )
    my_degrees = lax.dynamic_slice_in_dim(
        degree_table, lax.axis_index("level") * local_degrees, local_degrees
    )
    usable = my_degrees[None, :] >= my_orders[:, None]
    masked = jnp.where(usable[:, :, None, None, None], spectral, jnp.zeros((), jnp.bfloat16))
    vertical = jnp.einsum(
        "mnkrl,nql->mkrqn", masked, factors, preferred_element_type=jnp.float32
    ).astype(jnp.bfloat16)
    leg_aligned = jnp.take(legendre, degree_table, axis=1)
    fields = jnp.einsum(
        "mkrqn,mnl->lkrqm",
        lax.all_to_all(vertical, "level", split_axis=3, concat_axis=4, tiled=True),
        leg_aligned,
        preferred_element_type=jnp.float32,
    ).astype(jnp.bfloat16)
    grid_points = jnp.arange(points, dtype=jnp.int32)
    phase_index = order_table[:, None] * grid_points[None, :] % points
    phase = phase_index.astype(jnp.float32) * (2.0 * jnp.pi / points)
    weight = jnp.where(order_table == 0, 1.0, 2.0).astype(jnp.float32)[:, None]
    fourier_table = jnp.stack([weight * jnp.cos(phase), -weight * jnp.sin(phase)]).astype(
        jnp.bfloat16
    )
    sigma_wide = sigma.astype(jnp.float32)[:, None]
    summed = jnp.einsum(
        "lkrqm,rmx->lkqx",
        lax.all_to_all(fields, "order", split_axis=0, concat_axis=4, tiled=True),
        fourier_table,
        preferred_element_type=jnp.float32,
    )
    return (summed * sigma_wide).astype(jnp.bfloat16)


def solution(mesh):
    return jax.shard_map(
        per_device,
        mesh=mesh,
        in_specs=(
            P("order", "level", None, None, None),
            P("level", None, None),
            P("order", None, None),
            P("order", "level", None),
            P(),
            P(),
        ),
        out_specs=P("order", None, "level", None),
        check_vma=False,
    )
```

profile of v0, /device:TPU:1, one launch (start us, length us, event | category | flops | bytes accessed | tf_op | source)
XLA Modules:
  0.0 131.0 jit_solution(18221975622484884860)
XLA Ops:
  0.0 0.8 dynamic_slice.7
  0.8 0.8 dynamic_slice.6
  1.6 0.1 broadcast_compare_fusion
  1.6 1.4 %broadcast_select_fusion = bf16[16,16,2,2,128]{4,3,2,1,0:T(2,128)(2,1)S(1)} fusion(bf16[16,16,2,2,128]{4,3,2,1,0:T(2,128)(2,1)} %param.6, pred[16,16]{1,0:T(8,128)(4,1)S(1)} %broadcast_compare_fusion), kind=kLoop, calls=%fused_computation.26 | loop fusion | flops 131072 | bytes 524544 | tf_op jit(solution)/shard_map/jit(_where)/select_n | solution.py:18
  3.0 0.0 copy-done
  3.0 0.0 copy-start.2
  3.1 0.5 fusion.14
  3.5 1.9 %copy.33 = bf16[16,2,2,128,16]{0,2,1,4,3:T(2,128)(2,1)S(1)} copy(bf16[16,2,2,128,16]{3,0,2,1,4:T(8,128)(2,1)S(1)} %fusion.14) | data formatting | bytes 524288 | tf_op jit(solution)/shard_map/convert_element_type | solution.py:21
  5.4 2.9 %reshape.169 = bf16[32,2,2048]{2,1,0:T(2,128)(2,1)} reshape(bf16[128,16,2,2,16]{4,3,2,1,0:T(2,128)(2,1)S(1)} %bitcast.56) | data formatting | bytes 524288
  8.3 32.6 %all-to-all-start = ((bf16[32,2,2048]{2,1,0:T(2,128)(2,1)}), bf16[32,2,2048]{2,1,0:T(2,128)(2,1)S(1)}, u32[]{:S(2)}, u32[]{:S(2)}) async-start(bf16[32,2,2048]{2,1,0:T(2,128)(2,1)} %reshape.169), calls=%async_computation | async-start | bytes 524288 | tf_op jit(solution)/shard_map/all_to_all | solution.py:25
  41.0 12.0 %gather_fusion = bf16[512,16,256]{2,0,1:T(8,128)(2,1)} fusion(bf16[16,512,256]{2,1,0:T(8,128)(2,1)} %param.8, s32[1024]{0:T(1024)S(1)} %pad_clamp_fusion), kind=kCustom, calls=%fused_computation | custom fusion | bytes 8390656 | tf_op jit(solution)/shard_map/jit(_take)/gather | solution.py:22
  53.0 22.9 %all-to-all-done = bf16[32,2,2048]{2,1,0:T(2,128)(2,1)S(1)} async-done(((bf16[32,2,2048]{2,1,0:T(2,128)(2,1)}), bf16[32,2,2048]{2,1,0:T(2,128)(2,1)S(1)}, u32[]{:S(2)}, u32[]{:S(2)}) %all-to-all-start) | async-done | bytes 262176 | tf_op jit(solution)/shard_map/all_to_all | solution.py:25
  75.9 1.4 %reshape.170 = bf16[128,16,2,2,16]{4,3,2,1,0:T(2,128)(2,1)S(1)} reshape(bf16[32,2,2048]{2,1,0:T(2,128)(2,1)S(1)} %all-to-all-done) | data formatting | bytes 524288
  77.3 4.0 %copy.34 = bf16[16,2,2,128,16]{4,0,3,2,1:T(8,128)(2,1)} copy(bf16[16,2,2,128,16]{0,2,1,4,3:T(2,128)(2,1)S(1)} %bitcast.57) | data formatting | bytes 524288 | tf_op jit(solution)/shard_map/all_to_all | solution.py:25
  81.3 2.9 %copy.47 = bf16[16,2,2,4,32,16]{5,4,3,2,1,0:T(8,128)(2,1)S(1)} copy(bf16[16,2,2,4,32,16]{5,0,3,4,2,1:T(8,128)(2,1)} %bitcast.58) | data formatting | bytes 524288 | tf_op jit(solution)/shard_map/all_to_all | solution.py:25
  84.3 2.3 %reshape.167 = bf16[16,2,2,4,512]{4,3,2,1,0:T(4,128)(2,1)S(1)} reshape(bf16[16,2,2,4,32,16]{5,4,3,2,1,0:T(8,128)(2,1)S(1)} %copy.47) | data formatting | bytes 524288 | tf_op jit(solution)/shard_map/all_to_all | solution.py:25
  86.6 0.0 copy-start.1
  86.6 0.0 copy-start.3
  86.6 3.3 %fusion.18 = bf16[256,2,2,4,16]{0,3,2,1,4:T(4,128)(2,1)S(1)} fusion(bf16[16,2,2,4,512]{4,3,2,1,0:T(4,128)(2,1)S(1)} %reshape.167, bf16[512,16,256]{2,0,1:T(8,128)(2,1)} %gather_fusion, pred[512]{0:T(512)(128)(4,1)S(1)} %compare_and_fusion), kind=kOutput, calls=%fused_computation.23 | convolution fusion | flops 69271552 | bytes 4588032 | tf_op jit(solution)/shard_map/mkrqn,mnl->lkrqm/dot_general | solution.py:23
  89.9 1.0 copy.37
  90.9 1.8 %reshape.171 = bf16[32,2,1024]{2,1,0:T(2,128)(2,1)} reshape(bf16[256,2,2,4,16]{4,3,2,1,0:T(4,128)(2,1)S(1)} %copy.37) | data formatting | bytes 262144
  92.7 17.1 %all-to-all-start.1 = ((bf16[32,2,1024]{2,1,0:T(2,128)(2,1)}), bf16[32,2,1024]{2,1,0:T(2,128)(2,1)S(1)}, u32[]{:S(2)}, u32[]{:S(2)}) async-start(bf16[32,2,1024]{2,1,0:T(2,128)(2,1)} %reshape.171), calls=%async_computation.1 | async-start | bytes 262144 | tf_op jit(solution)/shard_map/all_to_all | solution.py:39
  109.8 0.0 copy-done.1
  109.8 0.0 copy-done.3
  109.8 15.2 %multiply_convert_fusion.1 = (bf16[1,512,1536]{2,1,0:T(8,128)(2,1)S(1)}, bf16[1,512,1536]{2,1,0:T(8,128)(2,1)}) fusion(s32[512]{0:T(512)S(1)} %copy-done.3, f32[512]{0:T(512)S(1)} %get-tuple-element.7, f32[512]{0:T(512)S(1)} %get-tuple-element.8), kind=kLoop, calls=%fused_computation.10 | loop fusion | flops 10223616 | bytes 3151872 | tf_op jit(solution)/shard_map/convert
  125.1 0.0 all-to-all-done.1
  125.1 0.7 reshape.172
  125.8 0.3 copy.54
  126.1 0.2 copy.48
  126.3 1.8 %reshape.168 = bf16[8,2,2,4,512]{4,0,2,3,1:T(8,128)(2,1)S(1)} reshape(bf16[8,2,2,4,32,16]{5,4,0,2,3,1:T(8,128)(2,1)S(1)} %copy.48) | data formatting | bytes 262144 | tf_op jit(solution)/shard_map/all_to_all | solution.py:39
  128.1 2.1 %fusion.12 = bf16[8,2,4,1536]{3,0,2,1:T(8,128)(2,1)S(1)} fusion(bf16[8,2,2,4,512]{4,0,2,3,1:T(8,128)(2,1)S(1)} %reshape.168, bf16[1,512,1536]{2,1,0:T(8,128)(2,1)} %get-tuple-element.6, bf16[1,512,1536]{2,1,0:T(8,128)(2,1)S(1)} %get-tuple-element.5, f32[8,4,1536]{2,0,1:T(8,128)S(1)} %copy.41), kind=kOutput, calls=%fused_computation.18 | convolution fusion | flops 203096064 | bytes 3670016 | tf_op jit(solution)/shard_map/lkrqm,rmx->lkqx/dot_general | solution.py:37
  130.2 0.8 copy.42
  (7 shorter events, 0.0 us)
Async XLA Ops:
  0.0 3.0 %copy-start = (bf16[16,128,128]{2,1,0:T(8,128)(2,1)S(1)}, bf16[16,128,128]{2,1,0:T(8,128)(2,1)}, u32[]{:S(2)}) copy-start(bf16[16,128,128]{2,1,0:T(8,128)(2,1)} %param.7) | copy-start | bytes 1572868
  3.0 37.9 %copy-start.2 = (s32[512]{0:T(512)S(1)}, s32[512]{0:T(512)}, u32[]{:S(2)}) copy-start(s32[512]{0:T(512)} %param.11) | copy-start | bytes 6148
  8.3 67.6 %all-to-all-start = ((bf16[32,2,2048]{2,1,0:T(2,128)(2,1)}), bf16[32,2,2048]{2,1,0:T(2,128)(2,1)S(1)}, u32[]{:S(2)}, u32[]{:S(2)}) async-start(bf16[32,2,2048]{2,1,0:T(2,128)(2,1)} %reshape.169), calls=%async_computation | async-start | bytes 524288 | tf_op jit(solution)/shard_map/all_to_all | solution.py:25
  86.6 23.2 %copy-start.1 = (bf16[8,4,1536]{2,1,0:T(4,128)(2,1)S(1)}, bf16[8,4,1536]{2,1,0:T(4,128)(2,1)}, u32[]{:S(2)}) copy-start(bf16[8,4,1536]{2,1,0:T(4,128)(2,1)} %param.9) | copy-start | bytes 294916
  86.6 23.2 %copy-start.3 = (s32[512]{0:T(512)S(1)}, s32[512]{0:T(512)}, u32[]{:S(2)}) copy-start(s32[512]{0:T(512)} %param.10) | copy-start | bytes 6148
  92.7 32.4 %all-to-all-start.1 = ((bf16[32,2,1024]{2,1,0:T(2,128)(2,1)}), bf16[32,2,1024]{2,1,0:T(2,128)(2,1)S(1)}, u32[]{:S(2)}, u32[]{:S(2)}) async-start(bf16[32,2,1024]{2,1,0:T(2,128)(2,1)} %reshape.171), calls=%async_computation.1 | async-start | bytes 262144 | tf_op jit(solution)/shard_map/all_to_all | solution.py:39
where the time goes:
time: 131 us
  starting transfers between devices  49.7 us (38%)
  local copies, waits for them, and re-layouts  35.6 us (27%)
  waiting for transfers between devices  22.9 us (17%)
  other arithmetic  16.7 us (13%)
  matrix products  5.82 us (4%)
    all_to_all x1, starting transfers between devices, per_device(): lax.all_to_all(vertical, 'level', split_axis=3, concat_axis=4, tiled=True)  32.6 us
    all_to_all x1, waiting for transfers between devices, per_device(): lax.all_to_all(vertical, 'level', split_axis=3, concat_axis=4, tiled=True)  22.9 us
    all_to_all x1, starting transfers between devices, per_device(): lax.all_to_all(fields, 'order', split_axis=0, concat_axis=4, tiled=True)  17.1 us
    another operation x1, other arithmetic  15.2 us
    gather x1, local copies, waits for them, and re-layouts, per_device(): leg_aligned = jnp.take(legendre, degree_table, axis=1)  12 us
    all_to_all x3, local copies, waits for them, and re-layouts, per_device(): lax.all_to_all(vertical, 'level', split_axis=3, concat_axis=4, tiled=True)  9.28 us
    unnamed x12, local copies, waits for them, and re-layouts  6.8 us
    dot_general x1, matrix products, per_device(): jnp.einsum('mkrqn,mnl->lkrqm', lax.all_to_all(vertical, 'level', split_ax...  3.26 us
  transfers between devices with their start and end apart: 2, of which 1 were waited for; matrix products, arithmetic and copies ran while one was open for 21% of the time, Pallas kernels for 0%

commit v1 on v0

v1 whole, which is shorter than its diff:
```python
import jax
import jax.numpy as jnp
from jax import lax
from jax.experimental import pallas as pl
from jax.experimental.pallas import tpu as pltpu
from jax.sharding import PartitionSpec as P

F32 = jnp.float32
BF16 = jnp.bfloat16
VMEM = pl.BlockSpec(memory_space=pltpu.VMEM)
HBM = pl.BlockSpec(memory_space=pltpu.HBM)


def in_hbm(x):
    return pltpu.with_memory_space_constraint(x, pltpu.HBM)


def params(mib):
    return pltpu.CompilerParams(vmem_limit_bytes=mib * 2**20)


def vertical_kernel(ord_hbm, deg_hbm, spec_hbm, fac_hbm, out_ref, ords, degs, spec, fac, x32, v32, w32, sems):
    orders, degrees, parts = 16, 16, 4
    per = degrees // parts
    copies = [
        pltpu.make_async_copy(spec_hbm, spec, sems.at[0]),
        pltpu.make_async_copy(ord_hbm, ords, sems.at[1]),
        pltpu.make_async_copy(deg_hbm, degs, sems.at[2]),
    ] + [
        pltpu.make_async_copy(
            fac_hbm.at[pl.ds(t * per, per)], fac.at[pl.ds(t * per, per)], sems.at[3 + t]
        )
        for t in range(parts)
    ]
    for copy in copies:
        copy.start()
    first_order = lax.axis_index("order") * orders
    first_degree = lax.axis_index("level") * degrees
    row = lax.broadcasted_iota(jnp.int32, (orders, 128), 0)
    low = lax.broadcasted_iota(jnp.int32, (32, 128), 1) < 64
    for copy in copies[:3]:
        copy.wait()
    x32[...] = spec[...].astype(F32)
    held = jnp.zeros((orders, 128), jnp.int32)
    for i in range(orders):
        held = jnp.where(row == i, ords[first_order + i], held)
    for j in range(degrees):
        if j % per == 0:
            copies[3 + j // per].wait()
        keep = held <= degs[first_degree + j]
        blocks = [
            jnp.where(keep, x32[pl.ds(j * 4 + p, orders, stride=4 * degrees), :], 0.0)
            for p in range(4)
        ]
        xj = jnp.concatenate(blocks + blocks, axis=0).astype(BF16)
        v32[j] = lax.dot_general(
            fac[j], xj, (((1,), (1,)), ((), ())), preferred_element_type=F32
        )
    for j in range(degrees):
        s = [v32[j, pl.ds(q, 32, stride=4), :] for q in range(4)]
        w32[0, pl.ds(j, 32, stride=degrees), :] = jnp.where(low, s[0], s[1])
        w32[1, pl.ds(j, 32, stride=degrees), :] = jnp.where(low, s[2], s[3])
    out_ref[:, 0:128] = w32[0].astype(BF16)
    out_ref[:, 128:256] = w32[1].astype(BF16)


def align_kernel(deg_ref, leg_ref, out_ref, onehot):
    @pl.when(pl.program_id(0) == 0)
    def _():
        degree = lax.broadcasted_iota(jnp.int32, onehot.shape, 0)
        onehot[...] = jnp.where(degree == deg_ref[...], 1.0, 0.0).astype(BF16)

    slots = onehot.shape[1]
    for i in range(leg_ref.shape[0]):
        out_ref[0, :, i * slots : (i + 1) * slots] = lax.dot_general(
            leg_ref[i], onehot[...], (((0,), (0,)), ((), ())), preferred_element_type=F32
        ).astype(BF16)


def table_kernel(ca_ref, sa_ref, cb_ref, sb_ref, out_ref):
    cb, sb = cb_ref[...], sb_ref[...]
    rows = cb.shape[0]
    per = out_ref.shape[2] // 128
    for a in range(out_ref.shape[0] * per):
        ca, sa = ca_ref[:, a : a + 1], sa_ref[:, a : a + 1]
        lanes = slice((a % per) * 128, (a % per + 1) * 128)
        out_ref[a // per, 0:rows, lanes] = (ca * cb - sa * sb).astype(BF16)
        out_ref[a // per, rows : 2 * rows, lanes] = (-(sa * cb + ca * sb)).astype(BF16)


def legendre_kernel(leg_hbm, r_ref, out_ref, leg, sems):
    groups = leg.shape[0]
    copies = [pltpu.make_async_copy(leg_hbm.at[g], leg.at[g], sems.at[g]) for g in range(groups)]
    for copy in copies:
        copy.start()
    lane = lax.broadcasted_iota(jnp.int32, (1, r_ref.shape[1]), 1) % 16
    r = r_ref[...]
    per = 16 // groups
    acc = jnp.zeros(out_ref.shape, F32)
    for g in range(groups):
        mine = [
            r * jnp.where(lane == g * per + i, 1.0, 0.0).astype(BF16) for i in range(per)
        ]
        rows = jnp.concatenate(mine, axis=0)
        copies[g].wait()
        acc += jnp.dot(leg[g], rows, preferred_element_type=F32)
    out_ref[...] = acc.astype(BF16)


def grid_kernel(r_ref, four_hbm, sig_hbm, out_ref, four, sig, lhs32, sems):
    chunks = four.shape[0]
    copies = [pltpu.make_async_copy(four_hbm.at[t], four.at[t], sems.at[t]) for t in range(chunks)]
    copies.append(pltpu.make_async_copy(sig_hbm, sig, sems.at[chunks]))
    for copy in copies:
        copy.start()
    block = lax.broadcasted_iota(jnp.int32, (8, 128), 1) // 16
    for g in range(4):
        for half in range(2):
            v = [
                r_ref[(g * 8 + t) * 8 : (g * 8 + t + 1) * 8, half * 128 : (half + 1) * 128].astype(F32)
                for t in range(8)
            ]
            for s in (1, 2, 4):
                first = (block & s) == 0
                for t in range(8):
                    if t & s:
                        continue
                    a, b = v[t], v[t + s]
                    v[t] = jnp.where(first, a, pltpu.roll(b, s * 16, 1))
                    v[t + s] = jnp.where(first, pltpu.roll(a, 128 - s * 16, 1), b)
            for cl in range(8):
                c = half * 8 + cl
                q, k, r = c // 4, (c // 2) % 2, c % 2
                lhs32[r * 4 + g, pl.ds(k * 4 + q, 8, stride=8), :] = v[cl]
    lhs = jnp.concatenate([lhs32[t].astype(BF16) for t in range(8)], axis=1)
    copies[chunks].wait()
    width = four.shape[2]
    for t in range(chunks):
        copies[t].wait()
        acc = jnp.dot(lhs, four[t], preferred_element_type=F32)
        res = (acc * sig[:, t * width : (t + 1) * width]).astype(BF16)
        for u in range(16):
            out_ref[u // 2, u % 2, :, t * width : (t + 1) * width] = res[u * 4 : (u + 1) * 4, :]


def per_device(spectral, factors, legendre, sigma, order_table, degree_table):
    lats, levs, points = sigma.shape
    waves = order_table.shape[0]
    dma = pltpu.SemaphoreType.DMA
    send = pl.pallas_call(
        vertical_kernel,
        out_shape=jax.ShapeDtypeStruct((512, 256), BF16),
        in_specs=[HBM] * 4,
        out_specs=VMEM,
        scratch_shapes=[
            pltpu.SMEM((waves,), jnp.int32),
            pltpu.SMEM((waves,), jnp.int32),
            pltpu.VMEM((1024, 128), BF16),
            pltpu.VMEM((16, 128, 128), BF16),
            pltpu.VMEM((1024, 128), F32),
            pltpu.VMEM((16, 128, 128), F32),
            pltpu.VMEM((2, 512, 128), F32),
            dma((7,)),
        ],
        compiler_params=params(8),
        name="vertical",
    )(in_hbm(order_table), in_hbm(degree_table), in_hbm(spectral.reshape(1024, 128)), in_hbm(factors))
    got = lax.all_to_all(send, "level", split_axis=0, concat_axis=0, tiled=True)

    per = 4
    aligned = pl.pallas_call(
        align_kernel,
        out_shape=jax.ShapeDtypeStruct((16 // per, 256, per * 512), BF16),
        grid=(16 // per,),
        in_specs=[
            pl.BlockSpec((1, 512), lambda i: (0, 0)),
            pl.BlockSpec((per, 512, 256), lambda i: (i, 0, 0)),
        ],
        out_specs=pl.BlockSpec((1, 256, per * 512), lambda i: (i, 0, 0)),
        scratch_shapes=[pltpu.VMEM((512, 512), BF16)],
        compiler_params=params(16),
        name="align",
    )(degree_table.reshape(1, waves), in_hbm(legendre))

    step = jnp.arange(128, dtype=jnp.int32)[None, :]
    m = order_table[:, None]
    weight = jnp.where(m == 0, 1.0, 2.0).astype(F32)
    phase_b = ((m * step) % points).astype(F32) * (2.0 * jnp.pi / points)
    phase_a = ((m * (step % 12)) % 12).astype(F32) * (2.0 * jnp.pi / 12)
    fourier = pl.pallas_call(
        table_kernel,
        out_shape=jax.ShapeDtypeStruct((3, 2 * waves, points // 3), BF16),
        in_specs=[VMEM] * 4,
        out_specs=VMEM,
        compiler_params=params(8),
        name="table",
    )(jnp.cos(phase_a), jnp.sin(phase_a), weight * jnp.cos(phase_b), weight * jnp.sin(phase_b))
    sig = jnp.broadcast_to(sigma.astype(F32)[:, None], (lats, 2, levs, points)).reshape(64, points)
    got, aligned, fourier, sig = lax.optimization_barrier((got, aligned, fourier, sig))

    fields = pl.pallas_call(
        legendre_kernel,
        out_shape=jax.ShapeDtypeStruct((256, 256), BF16),
        in_specs=[HBM, VMEM],
        out_specs=VMEM,
        scratch_shapes=[pltpu.VMEM((4, 256, 2048), BF16), dma((4,))],
        compiler_params=params(8),
        name="legendre",
    )(in_hbm(aligned), got)
    got2 = lax.all_to_all(fields, "order", split_axis=0, concat_axis=0, tiled=True)
    return pl.pallas_call(
        grid_kernel,
        out_shape=jax.ShapeDtypeStruct((lats, 2, levs, points), BF16),
        in_specs=[VMEM, HBM, HBM],
        out_specs=VMEM,
        scratch_shapes=[
            pltpu.VMEM((3, 1024, 512), BF16),
            pltpu.VMEM((64, 1536), F32),
            pltpu.VMEM((8, 64, 128), F32),
            dma((4,)),
        ],
        compiler_params=params(8),
        name="grid",
    )(got2, in_hbm(fourier), in_hbm(sig))


def solution(mesh):
    return jax.shard_map(
        per_device,
        mesh=mesh,
        in_specs=(
            P("order", "level", None, None, None),
            P("level", None, None),
            P("order", None, None),
            P("order", "level", None),
            P(),
            P(),
        ),
        out_specs=P("order", None, "level", None),
        check_vma=False,
    )
```

time: 131 us -> 108 us (0.82); the launches traced: 131 us -> 107 us
  local copies, waits for them, and re-layouts: 35.6 us -> 6.1 us
  blocking collectives: 0 us -> 28.5 us
  Pallas kernels: 0 us -> 17.3 us
  starting transfers between devices: 49.7 us -> 32.6 us
  other arithmetic: 16.7 us -> 2.21 us
  matrix products: 5.82 us -> 0 us
  waiting for transfers between devices: 22.9 us -> 19.8 us
    all_to_all x0 -> x1, blocking collectives: none -> 28.5 us  [per_device(): lax.all_to_all(fields, 'order', split_axis=0, concat_axis=0, tiled=True)]
    pallas_call x0 -> x5, Pallas kernels: none -> 17.3 us  [the longest x1 4.89 us: per_device(): pl.pallas_call(align_kernel, out_shape=jax.ShapeDtypeStruct((16 // per, 2...]
    all_to_all x2 -> x1, starting transfers between devices: 49.7 us -> 32.6 us  [per_device(): got = lax.all_to_all(send, 'level', split_axis=0, concat_axis=0, tiled=True)]
    another operation x1 -> x0, other arithmetic: 15.2 us -> none
    gather x1 -> x0, local copies, waits for them, and re-layouts: 12 us -> none  [per_device(): leg_aligned = jnp.take(legendre, degree_table, axis=1)]
    all_to_all x6 -> x0, local copies, waits for them, and re-layouts: 11.6 us -> none  [the longest x3 9.28 us: per_device(): lax.all_to_all(vertical, 'level', split_axis=3, concat_axis=4, tiled=True)]
    dot_general x3 -> x0, matrix products: 5.82 us -> none  [the longest x1 3.26 us: per_device(): jnp.einsum('mkrqn,mnl->lkrqm', lax.all_to_all(vertical, 'level', split_ax...]
    convert_element_type x4 -> x0, local copies, waits for them, and re-layouts: 3.69 us -> none  [the longest x1 1.9 us: per_device(): vertical = jnp.einsum('mnkrl,nql->mkrqn', masked, factors, preferred_elem...]
  transfers between devices with their start and end apart: 2 -> 1, of which waited for: 1 -> 1; matrix products, arithmetic and copies ran while one was open for 21% -> 4% of each run, Pallas kernels for 0% -> 6%
where the time goes in v1:
time: 108 us; the launch traced here: 107 us
  starting transfers between devices  32.6 us (30%)
  blocking collectives  28.5 us (26%)
  waiting for transfers between devices  19.8 us (18%)
  Pallas kernels  17.3 us (16%)
  local copies, waits for them, and re-layouts  6.1 us (6%)
  other arithmetic  2.21 us (2%)
    all_to_all x1, starting transfers between devices, per_device(): got = lax.all_to_all(send, 'level', split_axis=0, concat_axis=0, tiled=True)  32.6 us
    all_to_all x1, blocking collectives, per_device(): lax.all_to_all(fields, 'order', split_axis=0, concat_axis=0, tiled=True)  28.5 us
    all_to_all x1, waiting for transfers between devices, per_device(): got = lax.all_to_all(send, 'level', split_axis=0, concat_axis=0, tiled=True)  19.8 us
    pallas_call x1, Pallas kernels, per_device(): pl.pallas_call(align_kernel, out_shape=jax.ShapeDtypeStruct((16 // per, 2...  4.89 us
    unnamed x8, local copies, waits for them, and re-layouts  4.29 us
    pallas_call x1, Pallas kernels, per_device(): pl.pallas_call(legendre_kernel, out_shape=jax.ShapeDtypeStruct((256, 256)...  4.11 us
    pallas_call x1, Pallas kernels, per_device(): pl.pallas_call(grid_kernel, out_shape=jax.ShapeDtypeStruct((lats, 2, levs...  3.56 us
    pallas_call x1, Pallas kernels, per_device(): pl.pallas_call(vertical_kernel, out_shape=jax.ShapeDtypeStruct((512, 256)...  2.84 us
  transfers between devices with their start and end apart: 1, of which 1 were waited for; matrix products, arithmetic and copies ran while one was open for 4% of the time, Pallas kernels for 6%

profile of v1, /device:TPU:1, one launch (start us, length us, event | category | flops | bytes accessed | tf_op | source)
XLA Modules:
  0.0 106.6 jit_solution(5859087627381620263)
XLA Ops:
  0.0 2.8 %vertical.1 = bf16[512,256]{1,0:T(8,128)(2,1)} custom-call(s32[512]{0:T(512)} %ord_hbm.1, s32[512]{0:T(512)} %deg_hbm.1, bf16[1024,128]{1,0:T(8,128)(2,1)} %bitcast.10, bf16[16,128,128]{2,1,0:T(8,128)(2,1)} %fac_hbm.1), custom_call_target="tpu_custom_call" | custom-call | tf_op jit(solution)/shard_map/vertical/pallas_call | solution.py:150
  2.9 32.6 %all-to-all-start = ((bf16[32,16,256]{2,1,0:T(8,128)(2,1)}), bf16[32,16,256]{2,1,0:T(8,128)(2,1)S(1)}, u32[]{:S(2)}, u32[]{:S(2)}) async-start(bf16[32,16,256]{2,1,0:T(8,128)(2,1)} %bitcast.1), calls=%async_computation | async-start | bytes 524288 | tf_op jit(solution)/shard_map/all_to_all | solution.py:168
  35.5 0.9 broadcast_in_dim.18
  36.4 0.9 reshape.35.sig_hbm
  37.3 0.0 copy-start.2
  37.3 0.7 copy-done.2
  38.0 0.0 copy-start.3
  38.0 4.9 %align.1.leg_hbm = bf16[4,256,2048]{2,1,0:T(8,128)(2,1)S(1)} custom-call(s32[1,512]{1,0:T(1,128)S(1)} %bitcast.9, bf16[16,512,256]{2,1,0:T(8,128)(2,1)} %leg_ref.1), custom_call_target="tpu_custom_call" | custom-call | tf_op jit(solution)/shard_map/align/pallas_call | solution.py:171
  42.9 0.0 copy-start
  42.9 1.9 %copy-done = bf16[4,256,2048]{2,1,0:T(8,128)(2,1)} copy-done((bf16[4,256,2048]{2,1,0:T(8,128)(2,1)}, bf16[4,256,2048]{2,1,0:T(8,128)(2,1)S(1)}, u32[]{:S(2)}) %copy-start) | copy-done | bytes 4194328
  44.8 0.0 copy-done.3
  44.9 2.2 %sine_multiply_fusion = (f32[512,128]{1,0:T(8,128)S(1)}, f32[512,128]{1,0:T(8,128)S(1)}, f32[512,128]{1,0:T(8,128)S(1)}, f32[512,128]{1,0:T(8,128)S(1)}) fusion(f32[512]{0:T(512)S(1)} %compare_select_fusion, s32[512]{0:T(512)S(1)} %copy-done.3, s32[128]{0:T(128)S(1)} %and_select_fusion), kind=kLoop, calls=%fused_computation.6 | loop fusion | flops 1310720 | bytes 1053184 | tf_op jit(solution)/shard_map/mul | solution.py:197
  47.1 1.9 %table.1.four_hbm = bf16[3,1024,512]{2,1,0:T(8,128)(2,1)S(1)} custom-call(f32[512,128]{1,0:T(8,128)S(1)} %get-tuple-element.17.ca_ref, f32[512,128]{1,0:T(8,128)S(1)} %get-tuple-element.18.sa_ref, f32[512,128]{1,0:T(8,128)S(1)} %get-tuple-element.14.cb_ref, f32[512,128]{1,0:T(8,128)S(1)} %get-tuple-element.13.sb_ref), custom_call_target="tpu_custom_call" | custom-call | tf_op jit(solution)/shard_map/table/pallas_call | solution.py:190
  48.9 0.0 copy-start.1
  48.9 1.7 %copy-done.1 = bf16[3,1024,512]{2,1,0:T(8,128)(2,1)} copy-done((bf16[3,1024,512]{2,1,0:T(8,128)(2,1)}, bf16[3,1024,512]{2,1,0:T(8,128)(2,1)S(1)}, u32[]{:S(2)}) %copy-start.1) | copy-done | bytes 3145752
  50.6 19.8 %all-to-all-done = bf16[32,16,256]{2,1,0:T(8,128)(2,1)S(1)} async-done(((bf16[32,16,256]{2,1,0:T(8,128)(2,1)}), bf16[32,16,256]{2,1,0:T(8,128)(2,1)S(1)}, u32[]{:S(2)}, u32[]{:S(2)}) %all-to-all-start) | async-done | bytes 262176 | tf_op jit(solution)/shard_map/all_to_all | solution.py:168
  70.4 4.1 %legendre.1 = bf16[256,256]{1,0:T(8,128)(2,1)S(1)} custom-call(bf16[4,256,2048]{2,1,0:T(8,128)(2,1)} %copy-done, bf16[512,256]{1,0:T(8,128)(2,1)S(1)} %bitcast.6), custom_call_target="tpu_custom_call" | custom-call | tf_op jit(solution)/shard_map/legendre/pallas_call | solution.py:201
  74.5 28.5 %all_to_all.23 = bf16[32,8,256]{2,1,0:T(8,128)(2,1)S(1)} all-to-all(bf16[32,8,256]{2,1,0:T(8,128)(2,1)S(1)} %bitcast.7), channel_id=1, replica_groups=mesh['order'=32,'level'=32] {'order'}, dimensions={0} | all-to-all | bytes 262144 | tf_op jit(solution)/shard_map/all_to_all | solution.py:210
  103.0 3.6 %grid.1 = bf16[8,2,4,1536]{3,2,1,0:T(4,128)(2,1)} custom-call(bf16[256,256]{1,0:T(8,128)(2,1)S(1)} %bitcast.8, bf16[3,1024,512]{2,1,0:T(8,128)(2,1)} %copy-done.1, f32[64,1536]{1,0:T(8,128)} %reshape.35.sig_hbm), custom_call_target="tpu_custom_call" | custom-call | tf_op jit(solution)/shard_map/grid/pallas_call | solution.py:211
  (2 shorter events, 0.0 us)
Async XLA Ops:
  2.9 67.6 %all-to-all-start = ((bf16[32,16,256]{2,1,0:T(8,128)(2,1)}), bf16[32,16,256]{2,1,0:T(8,128)(2,1)S(1)}, u32[]{:S(2)}, u32[]{:S(2)}) async-start(bf16[32,16,256]{2,1,0:T(8,128)(2,1)} %bitcast.1), calls=%async_computation | async-start | bytes 524288 | tf_op jit(solution)/shard_map/all_to_all | solution.py:168
  37.3 0.7 copy-start.2
  38.0 6.9 %copy-start.3 = (s32[512]{0:T(512)S(1)}, s32[512]{0:T(512)}, u32[]{:S(2)}) copy-start(s32[512]{0:T(512)} %ord_hbm.1) | copy-start | bytes 6148
  42.9 1.9 %copy-start = (bf16[4,256,2048]{2,1,0:T(8,128)(2,1)}, bf16[4,256,2048]{2,1,0:T(8,128)(2,1)S(1)}, u32[]{:S(2)}) copy-start(bf16[4,256,2048]{2,1,0:T(8,128)(2,1)S(1)} %align.1.leg_hbm) | copy-start | bytes 12582916
  48.9 1.7 %copy-start.1 = (bf16[3,1024,512]{2,1,0:T(8,128)(2,1)}, bf16[3,1024,512]{2,1,0:T(8,128)(2,1)S(1)}, u32[]{:S(2)}) copy-start(bf16[3,1024,512]{2,1,0:T(8,128)(2,1)S(1)} %table.1.four_hbm) | copy-start | bytes 9437188

commit v2 on v1

--- a/solution.py
+++ b/solution.py
@@ -1,3 +1,5 @@
+import functools
+
 import jax
 import jax.numpy as jnp
 from jax import lax
@@ -8,11 +10,20 @@
 F32 = jnp.float32
 BF16 = jnp.bfloat16
 VMEM = pl.BlockSpec(memory_space=pltpu.VMEM)
+FIRST_LEVEL, FIRST_ORDER = 21, 19
 HBM = pl.BlockSpec(memory_space=pltpu.HBM)
+
+
+def place(first, i):
+    return first if i == 0 else 0 if i == first else i
 
 
 def in_hbm(x):
     return pltpu.with_memory_space_constraint(x, pltpu.HBM)
+
+
+def in_vmem(x):
+    return pltpu.with_memory_space_constraint(x, pltpu.VMEM)
 
 
 def params(mib):
@@ -62,22 +73,52 @@
         w32[1, pl.ds(j, 32, stride=degrees), :] = jnp.where(low, s[2], s[3])
     out_ref[:, 0:128] = w32[0].astype(BF16)
     out_ref[:, 128:256] = w32[1].astype(BF16)
-
-
-def align_kernel(deg_ref, leg_ref, out_ref, onehot):
-    @pl.when(pl.program_id(0) == 0)
+    for p in (0, FIRST_LEVEL):
+        d = place(FIRST_LEVEL, p) * degrees
+        rows = slice(p * degrees, (p + 1) * degrees)
+        out_ref[rows, 0:128] = w32[0, d : d + degrees, :].astype(BF16)
+        out_ref[rows, 128:256] = w32[1, d : d + degrees, :].astype(BF16)
+
+
+def align_kernel(kept, deg_ref, leg_ref, near_ref, far_ref, onehot):
+    step = pl.program_id(0)
+
+    @pl.when(step == 0)
     def _():
         degree = lax.broadcasted_iota(jnp.int32, onehot.shape, 0)
-        onehot[...] = jnp.where(degree == deg_ref[...], 1.0, 0.0).astype(BF16)
-
-    slots = onehot.shape[1]
+        a, b = FIRST_LEVEL * 16, FIRST_LEVEL * 16 + 16
+        held = jnp.concatenate(
+            [deg_ref[:, a:b], deg_ref[:, 16:a], deg_ref[:, 0:16], deg_ref[:, b:]], axis=1
+        )
+        onehot[...] = jnp.where(degree == held, 1.0, 0.0).astype(BF16)
+
     for i in range(leg_ref.shape[0]):
-        out_ref[0, :, i * slots : (i + 1) * slots] = lax.dot_general(
+        rows = lax.dot_general(
             leg_ref[i], onehot[...], (((0,), (0,)), ((), ())), preferred_element_type=F32
         ).astype(BF16)
 
-
-def table_kernel(ca_ref, sa_ref, cb_ref, sb_ref, out_ref):
+        @pl.when(step < kept)
+        def _():
+            for b in range(4):
+                near_ref[step, i * 4 + b] = rows[:, b * 128 : (b + 1) * 128]
+
+        @pl.when(step >= kept)
+        def _():
+            for b in range(4):
+                far_ref[0, i * 4 + b] = rows[:, b * 128 : (b + 1) * 128]
+
+
+def table_kernel(ca_hbm, sa_hbm, cb_hbm, sb_hbm, out_ref, ca_ref, sa_ref, cb_ref, sb_ref, sems):
+    copies = [
+        pltpu.make_async_copy(src, dst, sems.at[t])
+        for t, (src, dst) in enumerate(
+            [(cb_hbm, cb_ref), (sb_hbm, sb_ref), (ca_hbm, ca_ref), (sa_hbm, sa_ref)]
+        )
+    ]
+    for copy in copies:
+        copy.start()
+    for copy in copies:
+        copy.wait()
     cb, sb = cb_ref[...], sb_ref[...]
     rows = cb.shape[0]
     per = out_ref.shape[2] // 128
@@ -88,37 +129,42 @@
         out_ref[a // per, rows : 2 * rows, lanes] = (-(sa * cb + ca * sb)).astype(BF16)
 
 
-def legendre_kernel(leg_hbm, r_ref, out_ref, leg, sems):
-    groups = leg.shape[0]
-    copies = [pltpu.make_async_copy(leg_hbm.at[g], leg.at[g], sems.at[g]) for g in range(groups)]
+def legendre_kernel(near_ref, far_hbm, r_ref, out_ref, far, sems):
+    kept, left = near_ref.shape[0], far.shape[0]
+    copies = [pltpu.make_async_copy(far_hbm.at[g], far.at[g], sems.at[g]) for g in range(left)]
     for copy in copies:
         copy.start()
     lane = lax.broadcasted_iota(jnp.int32, (1, r_ref.shape[1]), 1) % 16
     r = r_ref[...]
-    per = 16 // groups
+    per = 16 // (kept + left)
     acc = jnp.zeros(out_ref.shape, F32)
-    for g in range(groups):
+    for g in range(kept + left):
         mine = [
             r * jnp.where(lane == g * per + i, 1.0, 0.0).astype(BF16) for i in range(per)
         ]
         rows = jnp.concatenate(mine, axis=0)
-        copies[g].wait()
-        acc += jnp.dot(leg[g], rows, preferred_element_type=F32)
+        if g >= kept:
+            copies[g - kept].wait()
+        src, at = (near_ref, g) if g < kept else (far, g - kept)
+        leg = jnp.concatenate([src[at, b] for b in range(src.shape[1])], axis=1)
+        acc += jnp.dot(leg, rows, preferred_element_type=F32)
     out_ref[...] = acc.astype(BF16)
-
-
-def grid_kernel(r_ref, four_hbm, sig_hbm, out_ref, four, sig, lhs32, sems):
+    for p in (0, FIRST_ORDER):
+        d = place(FIRST_ORDER, p) * 8
+        out_ref[p * 8 : (p + 1) * 8, :] = acc[d : d + 8, :].astype(BF16)
+
+
+def grid_kernel(r_ref, four, sig_hbm, out_hbm, sig, res_v, lhs32, sems):
     chunks = four.shape[0]
-    copies = [pltpu.make_async_copy(four_hbm.at[t], four.at[t], sems.at[t]) for t in range(chunks)]
-    copies.append(pltpu.make_async_copy(sig_hbm, sig, sems.at[chunks]))
-    for copy in copies:
-        copy.start()
+    copies = []
+    fetch = pltpu.make_async_copy(sig_hbm, sig, sems.at[chunks])
+    fetch.start()
     block = lax.broadcasted_iota(jnp.int32, (8, 128), 1) // 16
     for g in range(4):
         for half in range(2):
             v = [
-                r_ref[(g * 8 + t) * 8 : (g * 8 + t + 1) * 8, half * 128 : (half + 1) * 128].astype(F32)
-                for t in range(8)
+                r_ref[p * 8 : (p + 1) * 8, half * 128 : (half + 1) * 128].astype(F32)
+                for p in [place(FIRST_ORDER, g * 8 + t) for t in range(8)]
             ]
             for s in (1, 2, 4):
                 first = (block & s) == 0
@@ -133,14 +179,23 @@
                 q, k, r = c // 4, (c // 2) % 2, c % 2
                 lhs32[r * 4 + g, pl.ds(k * 4 + q, 8, stride=8), :] = v[cl]
     lhs = jnp.concatenate([lhs32[t].astype(BF16) for t in range(8)], axis=1)
-    copies[chunks].wait()
     width = four.shape[2]
     for t in range(chunks):
-        copies[t].wait()
+        if t == 0:
+            fetch.wait()
         acc = jnp.dot(lhs, four[t], preferred_element_type=F32)
-        res = (acc * sig[:, t * width : (t + 1) * width]).astype(BF16)
+        res = (acc * sig[:, t * width : (t + 1) * width].astype(F32)).astype(BF16)
         for u in range(16):
-            out_ref[u // 2, u % 2, :, t * width : (t + 1) * width] = res[u * 4 : (u + 1) * 4, :]
+            res_v[u // 2, u % 2, :, t * width : (t + 1) * width] = res[u * 4 : (u + 1) * 4, :]
+        lanes = pl.ds(t * width, width)
+        copies.append(
+            pltpu.make_async_copy(
+                res_v.at[:, :, :, lanes], out_hbm.at[:, :, :, lanes], sems.at[t]
+            )
+        )
+        copies[t].start()
+    for copy in copies:
+        copy.wait()
 
 
 def per_device(spectral, factors, legendre, sigma, order_table, degree_table):
@@ -149,7 +204,7 @@
     dma = pltpu.SemaphoreType.DMA
     send = pl.pallas_call(
         vertical_kernel,
-        out_shape=jax.ShapeDtypeStruct((512, 256), BF16),
+        out_shape=pltpu.VMEM((512, 256), BF16),
         in_specs=[HBM] * 4,
         out_specs=VMEM,
         scratch_shapes=[
@@ -165,20 +220,34 @@
         compiler_params=params(8),
         name="vertical",
     )(in_hbm(order_table), in_hbm(degree_table), in_hbm(spectral.reshape(1024, 128)), in_hbm(factors))
-    got = lax.all_to_all(send, "level", split_axis=0, concat_axis=0, tiled=True)
-
-    per = 4
-    aligned = pl.pallas_call(
-        align_kernel,
-        out_shape=jax.ShapeDtypeStruct((16 // per, 256, per * 512), BF16),
-        grid=(16 // per,),
+    got = lax.all_to_all(
+        send,
+        "level",
+        split_axis=0,
+        concat_axis=0,
+        tiled=True,
+        axis_index_groups=[[place(FIRST_LEVEL, i) for i in range(32)]],
+    )
+
+    per, kept = 2, 5
+    groups = 16 // per
+    near, far = pl.pallas_call(
+        functools.partial(align_kernel, kept),
+        out_shape=(
+            pltpu.VMEM((kept, per * 4, 256, 128), BF16),
+            jax.ShapeDtypeStruct((groups - kept, per * 4, 256, 128), BF16),
+        ),
+        grid=(groups,),
         in_specs=[
             pl.BlockSpec((1, 512), lambda i: (0, 0)),
             pl.BlockSpec((per, 512, 256), lambda i: (i, 0, 0)),
         ],
-        out_specs=pl.BlockSpec((1, 256, per * 512), lambda i: (i, 0, 0)),
+        out_specs=(
+            VMEM,
+            pl.BlockSpec((1, per * 4, 256, 128), lambda i: (jnp.maximum(i - kept, 0), 0, 0, 0)),
+        ),
         scratch_shapes=[pltpu.VMEM((512, 512), BF16)],
-        compiler_params=params(16),
+        compiler_params=params(12),
         name="align",
     )(degree_table.reshape(1, waves), in_hbm(legendre))
 
@@ -187,41 +256,59 @@
     weight = jnp.where(m == 0, 1.0, 2.0).astype(F32)
     phase_b = ((m * step) % points).astype(F32) * (2.0 * jnp.pi / points)
     phase_a = ((m * (step % 12)) % 12).astype(F32) * (2.0 * jnp.pi / 12)
+    tables = (
+        jnp.cos(phase_a),
+        jnp.sin(phase_a),
+        weight * jnp.cos(phase_b),
+        weight * jnp.sin(phase_b),
+    )
+    sig = jnp.broadcast_to(sigma[:, None], (lats, 2, levs, points)).reshape(64, points)
+    got, near, far, tables, sig = lax.optimization_barrier((got, near, far, tables, sig))
+
+    fields = pl.pallas_call(
+        legendre_kernel,
+        out_shape=pltpu.VMEM((256, 256), BF16),
+        in_specs=[VMEM, HBM, VMEM],
+        out_specs=VMEM,
+        scratch_shapes=[
+            pltpu.VMEM((groups - kept, per * 4, 256, 128), BF16),
+            dma((groups - kept,)),
+        ],
+        compiler_params=params(6),
+        name="legendre",
+    )(in_vmem(near), in_hbm(far), in_vmem(got))
+    fields, tables = lax.optimization_barrier((fields, tables))
     fourier = pl.pallas_call(
         table_kernel,
-        out_shape=jax.ShapeDtypeStruct((3, 2 * waves, points // 3), BF16),
-        in_specs=[VMEM] * 4,
+        out_shape=pltpu.VMEM((3, 2 * waves, points // 3), BF16),
+        in_specs=[HBM] * 4,
         out_specs=VMEM,
-        compiler_params=params(8),
+        scratch_shapes=[pltpu.VMEM((waves, 128), F32)] * 4 + [dma((4,))],
+        compiler_params=params(4),
         name="table",
-    )(jnp.cos(phase_a), jnp.sin(phase_a), weight * jnp.cos(phase_b), weight * jnp.sin(phase_b))
-    sig = jnp.broadcast_to(sigma.astype(F32)[:, None], (lats, 2, levs, points)).reshape(64, points)
-    got, aligned, fourier, sig = lax.optimization_barrier((got, aligned, fourier, sig))
-
-    fields = pl.pallas_call(
-        legendre_kernel,
-        out_shape=jax.ShapeDtypeStruct((256, 256), BF16),
-        in_specs=[HBM, VMEM],
-        out_specs=VMEM,
-        scratch_shapes=[pltpu.VMEM((4, 256, 2048), BF16), dma((4,))],
-        compiler_params=params(8),
-        name="legendre",
-    )(in_hbm(aligned), got)
-    got2 = lax.all_to_all(fields, "order", split_axis=0, concat_axis=0, tiled=True)
+    )(*[in_hbm(t) for t in tables])
+    got2 = lax.all_to_all(
+        fields,
+        "order",
+        split_axis=0,
+        concat_axis=0,
+        tiled=True,
+        axis_index_groups=[[place(FIRST_ORDER, i) for i in range(32)]],
+    )
     return pl.pallas_call(
         grid_kernel,
         out_shape=jax.ShapeDtypeStruct((lats, 2, levs, points), BF16),
-        in_specs=[VMEM, HBM, HBM],
-        out_specs=VMEM,
+        in_specs=[VMEM, VMEM, HBM],
+        out_specs=HBM,
         scratch_shapes=[
-            pltpu.VMEM((3, 1024, 512), BF16),
-            pltpu.VMEM((64, 1536), F32),
+            pltpu.VMEM((lats * 2 * levs, points), BF16),
+            pltpu.VMEM((lats, 2, levs, points), BF16),
             pltpu.VMEM((8, 64, 128), F32),
             dma((4,)),
         ],
-        compiler_params=params(8),
+        compiler_params=params(4),
         name="grid",
-    )(got2, in_hbm(fourier), in_hbm(sig))
+    )(in_vmem(got2), in_vmem(fourier), in_hbm(sig))
 
 
 def solution(mesh):

time: 108 us -> 87.4 us (0.81)
  blocking collectives: 28.5 us -> 0 us
  starting transfers between devices: 32.6 us -> 45.9 us
  waiting for transfers between devices: 19.8 us -> 15 us
  local copies, waits for them, and re-layouts: 6.1 us -> 3.52 us
  Pallas kernels: 17.3 us -> 19.2 us
  other arithmetic: 2.21 us -> 3.29 us
    all_to_all x1 -> x0, blocking collectives: 28.5 us -> none  [per_device(): lax.all_to_all(fields, 'order', split_axis=0, concat_axis=0, tiled=True)]
    all_to_all x1 -> x2, starting transfers between devices: 32.6 us -> 45.9 us  [the longest x1 37.6 us: per_device(): lax.all_to_all(send, 'level', split_axis=0, concat_axis=0, tiled=True, ax...]
    all_to_all x1 -> x2, waiting for transfers between devices: 19.8 us -> 15 us  [the longest x1 8.6 us: per_device(): lax.all_to_all(send, 'level', split_axis=0, concat_axis=0, tiled=True, ax...]
    pallas_call x4, Pallas kernels: 13.7 us -> 16.9 us  [the longest x1 7.99 us: per_device(): pl.pallas_call(functools.partial(align_kernel, kept), out_shape=(pltpu.VM...]
    unnamed x8 -> x6, local copies, waits for them, and re-layouts: 4.29 us -> 1.83 us
    pallas_call x1, Pallas kernels: 3.56 us -> 2.25 us  [per_device(): pl.pallas_call(grid_kernel, out_shape=jax.ShapeDtypeStruct((lats, 2, levs...]
    mul x1, other arithmetic: 2.2 us -> 3.28 us  [per_device(): weight * jnp.sin(phase_b)]
  transfers between devices with their start and end apart: 1 -> 2, of which waited for: 1 -> 2; matrix products, arithmetic and copies ran while one was open for 4% -> 6% of each run, Pallas kernels for 6% -> 13%
where the time goes in v2:
time: 87.4 us; the launch traced here: 86.9 us
  starting transfers between devices  45.9 us (53%)
  Pallas kernels  19.2 us (22%)
  waiting for transfers between devices  15 us (17%)
  local copies, waits for them, and re-layouts  3.52 us (4%)
  other arithmetic  3.29 us (4%)
    all_to_all x1, starting transfers between devices, per_device(): lax.all_to_all(send, 'level', split_axis=0, concat_axis=0, tiled=True, ax...  37.6 us
    all_to_all x1, waiting for transfers between devices, per_device(): lax.all_to_all(send, 'level', split_axis=0, concat_axis=0, tiled=True, ax...  8.6 us
    all_to_all x1, starting transfers between devices, per_device(): lax.all_to_all(fields, 'order', split_axis=0, concat_axis=0, tiled=True,...  8.24 us
    pallas_call x1, Pallas kernels, per_device(): pl.pallas_call(functools.partial(align_kernel, kept), out_shape=(pltpu.VM...  7.99 us
    all_to_all x1, waiting for transfers between devices, per_device(): lax.all_to_all(fields, 'order', split_axis=0, concat_axis=0, tiled=True,...  6.36 us
    mul x1, other arithmetic, per_device(): weight * jnp.sin(phase_b)  3.28 us
    pallas_call x1, Pallas kernels, per_device(): pl.pallas_call(table_kernel, out_shape=pltpu.VMEM((3, 2 * waves, points /...  3.08 us
    pallas_call x1, Pallas kernels, per_device(): pl.pallas_call(legendre_kernel, out_shape=pltpu.VMEM((256, 256), BF16), i...  3.02 us
  transfers between devices with their start and end apart: 2, of which 2 were waited for; matrix products, arithmetic and copies ran while one was open for 6% of the time, Pallas kernels for 13%

profile of v2, /device:TPU:1, one launch (start us, length us, event | category | flops | bytes accessed | tf_op | source)
XLA Modules:
  0.0 86.9 jit_solution(13277133191534625464)
XLA Ops:
  0.0 0.0 copy-start.2
  0.0 2.8 %vertical.1 = bf16[512,256]{1,0:T(8,128)(2,1)} custom-call(s32[512]{0:T(512)} %ord_hbm.1, s32[512]{0:T(512)} %deg_hbm.1, bf16[1024,128]{1,0:T(8,128)(2,1)} %bitcast.9, bf16[16,128,128]{2,1,0:T(8,128)(2,1)} %fac_hbm.1), custom_call_target="tpu_custom_call" | custom-call | tf_op jit(solution)/shard_map/vertical/pallas_call | solution.py:205
  2.9 37.6 %all-to-all-start = ((bf16[32,16,256]{2,1,0:T(8,128)(2,1)}), bf16[32,16,256]{2,1,0:T(8,128)(2,1)S(1)}, u32[]{:S(2)}, u32[]{:S(2)}) async-start(bf16[32,16,256]{2,1,0:T(8,128)(2,1)} %bitcast.1), calls=%async_computation | async-start | bytes 524288 | tf_op jit(solution)/shard_map/all_to_all | solution.py:223
  40.5 0.9 %broadcast_in_dim.18 = bf16[8,2,4,1536]{3,2,1,0:T(4,128)(2,1)S(1)} broadcast(bf16[8,4,1536]{2,1,0:T(4,128)(2,1)} %param.9), dimensions={0,2,3} | broadcast | bytes 294912 | tf_op jit(solution)/shard_map/broadcast_in_dim | solution.py:265
  41.5 0.7 reshape.35.sig_hbm
  42.2 0.0 copy-start.1
  42.2 0.7 copy-done.1
  42.9 8.0 %align.1 = (bf16[5,8,256,128]{3,2,1,0:T(8,128)(2,1)S(1)}, bf16[3,8,256,128]{3,2,1,0:T(8,128)(2,1)S(1)}) custom-call(s32[1,512]{1,0:T(1,128)S(1)} %bitcast.8, bf16[16,512,256]{2,1,0:T(8,128)(2,1)} %leg_ref.1), custom_call_target="tpu_custom_call" | custom-call | tf_op jit(solution)/shard_map/align/pallas_call | solution.py:234
  50.9 0.0 copy-start
  50.9 1.1 %copy-done = bf16[3,8,256,128]{3,2,1,0:T(8,128)(2,1)} copy-done((bf16[3,8,256,128]{3,2,1,0:T(8,128)(2,1)}, bf16[3,8,256,128]{3,2,1,0:T(8,128)(2,1)S(1)}, u32[]{:S(2)}) %copy-start) | copy-done | bytes 1572888
  52.0 0.0 copy-done.2
  52.1 3.3 %sine_multiply_fusion = (f32[512,128]{1,0:T(8,128)}, f32[512,128]{1,0:T(8,128)}, f32[512,128]{1,0:T(8,128)}, f32[512,128]{1,0:T(8,128)}) fusion(f32[512]{0:T(512)S(1)} %compare_select_fusion, s32[512]{0:T(512)S(1)} %copy-done.2, s32[128]{0:T(128)S(1)} %and_select_fusion), kind=kLoop, calls=%fused_computation.6 | loop fusion | flops 1310720 | bytes 1053184 | tf_op jit(solution)/shard_map/mul | solution.py:263
  55.3 8.6 %all-to-all-done = bf16[32,16,256]{2,1,0:T(8,128)(2,1)S(1)} async-done(((bf16[32,16,256]{2,1,0:T(8,128)(2,1)}), bf16[32,16,256]{2,1,0:T(8,128)(2,1)S(1)}, u32[]{:S(2)}, u32[]{:S(2)}) %all-to-all-start) | async-done | bytes 262176 | tf_op jit(solution)/shard_map/all_to_all | solution.py:223
  63.9 3.0 %legendre.1 = bf16[256,256]{1,0:T(8,128)(2,1)} custom-call(bf16[5,8,256,128]{3,2,1,0:T(8,128)(2,1)S(1)} %get-tuple-element.22.near_ref, bf16[3,8,256,128]{3,2,1,0:T(8,128)(2,1)} %copy-done, bf16[512,256]{1,0:T(8,128)(2,1)S(1)} %bitcast.6), custom_call_target="tpu_custom_call" | custom-call | tf_op jit(solution)/shard_map/legendre/pallas_call | solution.py:268
  67.0 8.2 %all-to-all-start.1 = ((bf16[32,8,256]{2,1,0:T(8,128)(2,1)}), bf16[32,8,256]{2,1,0:T(8,128)(2,1)S(1)}, u32[]{:S(2)}, u32[]{:S(2)}) async-start(bf16[32,8,256]{2,1,0:T(8,128)(2,1)} %bitcast.4), calls=%async_computation.1 | async-start | bytes 262144 | tf_op jit(solution)/shard_map/all_to_all | solution.py:290
  75.2 3.1 %table.1.four = bf16[3,1024,512]{2,1,0:T(8,128)(2,1)S(1)} custom-call(f32[512,128]{1,0:T(8,128)} %get-tuple-element.30.ca_hbm, f32[512,128]{1,0:T(8,128)} %get-tuple-element.31.sa_hbm, f32[512,128]{1,0:T(8,128)} %get-tuple-element.32.cb_hbm, f32[512,128]{1,0:T(8,128)} %get-tuple-element.33.sb_hbm), custom_call_target="tpu_custom_call" | custom-call | tf_op jit(solution)/shard_map/table/pallas_call | solution.py:281
  78.3 6.4 %all-to-all-done.1 = bf16[32,8,256]{2,1,0:T(8,128)(2,1)S(1)} async-done(((bf16[32,8,256]{2,1,0:T(8,128)(2,1)}), bf16[32,8,256]{2,1,0:T(8,128)(2,1)S(1)}, u32[]{:S(2)}, u32[]{:S(2)}) %all-to-all-start.1) | async-done | bytes 131104 | tf_op jit(solution)/shard_map/all_to_all | solution.py:290
  84.7 2.3 %grid.1 = bf16[8,2,4,1536]{3,2,1,0:T(4,128)(2,1)} custom-call(bf16[256,256]{1,0:T(8,128)(2,1)S(1)} %bitcast.7, bf16[3,1024,512]{2,1,0:T(8,128)(2,1)S(1)} %table.1.four, bf16[64,1536]{1,0:T(8,128)(2,1)} %reshape.35.sig_hbm), custom_call_target="tpu_custom_call" | custom-call | tf_op jit(solution)/shard_map/grid/pallas_call | solution.py:298
  (2 shorter events, 0.0 us)
Async XLA Ops:
  0.0 52.0 %copy-start.2 = (s32[512]{0:T(512)S(1)}, s32[512]{0:T(512)}, u32[]{:S(2)}) copy-start(s32[512]{0:T(512)} %ord_hbm.1) | copy-start | bytes 6148
  2.9 61.1 %all-to-all-start = ((bf16[32,16,256]{2,1,0:T(8,128)(2,1)}), bf16[32,16,256]{2,1,0:T(8,128)(2,1)S(1)}, u32[]{:S(2)}, u32[]{:S(2)}) async-start(bf16[32,16,256]{2,1,0:T(8,128)(2,1)} %bitcast.1), calls=%async_computation | async-start | bytes 524288 | tf_op jit(solution)/shard_map/all_to_all | solution.py:223
  42.2 0.7 copy-start.1
  50.9 1.1 %copy-start = (bf16[3,8,256,128]{3,2,1,0:T(8,128)(2,1)}, bf16[3,8,256,128]{3,2,1,0:T(8,128)(2,1)S(1)}, u32[]{:S(2)}) copy-start(bf16[3,8,256,128]{3,2,1,0:T(8,128)(2,1)S(1)} %get-tuple-element.23.far_hbm) | copy-start | bytes 4718596
  67.0 17.7 %all-to-all-start.1 = ((bf16[32,8,256]{2,1,0:T(8,128)(2,1)}), bf16[32,8,256]{2,1,0:T(8,128)(2,1)S(1)}, u32[]{:S(2)}, u32[]{:S(2)}) async-start(bf16[32,8,256]{2,1,0:T(8,128)(2,1)} %bitcast.4), calls=%async_computation.1 | async-start | bytes 262144 | tf_op jit(solution)/shard_map/all_to_all | solution.py:290

commit v3 on v2

--- a/solution.py
+++ b/solution.py
@@ -10,12 +10,15 @@
 F32 = jnp.float32
 BF16 = jnp.bfloat16
 VMEM = pl.BlockSpec(memory_space=pltpu.VMEM)
-FIRST_LEVEL, FIRST_ORDER = 21, 19
+LEVEL_GROUP = (
+    21, 0, 1, 2, 6, 3, 7, 4, 5, 8, 24, 9, 25, 10, 14, 26,
+    30, 11, 15, 27, 31, 12, 28, 13, 29, 16, 17, 18, 22, 19, 23, 20,
+)
+ORDER_GROUP = (
+    19, 7, 0, 6, 15, 31, 1, 5, 8, 14, 23, 24, 30, 2, 4, 9,
+    13, 16, 22, 25, 29, 3, 10, 12, 17, 21, 26, 28, 11, 18, 20, 27,
+)
 HBM = pl.BlockSpec(memory_space=pltpu.HBM)
-
-
-def place(first, i):
-    return first if i == 0 else 0 if i == first else i
 
 
 def in_hbm(x):
@@ -71,13 +74,10 @@
         s = [v32[j, pl.ds(q, 32, stride=4), :] for q in range(4)]
         w32[0, pl.ds(j, 32, stride=degrees), :] = jnp.where(low, s[0], s[1])
         w32[1, pl.ds(j, 32, stride=degrees), :] = jnp.where(low, s[2], s[3])
-    out_ref[:, 0:128] = w32[0].astype(BF16)
-    out_ref[:, 128:256] = w32[1].astype(BF16)
-    for p in (0, FIRST_LEVEL):
-        d = place(FIRST_LEVEL, p) * degrees
-        rows = slice(p * degrees, (p + 1) * degrees)
-        out_ref[rows, 0:128] = w32[0, d : d + degrees, :].astype(BF16)
-        out_ref[rows, 128:256] = w32[1, d : d + degrees, :].astype(BF16)
+    for p, d in enumerate(LEVEL_GROUP):
+        rows, source = slice(p * degrees, (p + 1) * degrees), slice(d * degrees, (d + 1) * degrees)
+        out_ref[rows, 0:128] = w32[0, source, :].astype(BF16)
+        out_ref[rows, 128:256] = w32[1, source, :].astype(BF16)
 
 
 def align_kernel(kept, deg_ref, leg_ref, near_ref, far_ref, onehot):
@@ -86,10 +86,7 @@
     @pl.when(step == 0)
     def _():
         degree = lax.broadcasted_iota(jnp.int32, onehot.shape, 0)
-        a, b = FIRST_LEVEL * 16, FIRST_LEVEL * 16 + 16
-        held = jnp.concatenate(
-            [deg_ref[:, a:b], deg_ref[:, 16:a], deg_ref[:, 0:16], deg_ref[:, b:]], axis=1
-        )
+        held = jnp.concatenate([deg_ref[:, d * 16 : (d + 1) * 16] for d in LEVEL_GROUP], axis=1)
         onehot[...] = jnp.where(degree == held, 1.0, 0.0).astype(BF16)
 
     for i in range(leg_ref.shape[0]):
@@ -148,10 +145,8 @@
         src, at = (near_ref, g) if g < kept else (far, g - kept)
         leg = jnp.concatenate([src[at, b] for b in range(src.shape[1])], axis=1)
         acc += jnp.dot(leg, rows, preferred_element_type=F32)
-    out_ref[...] = acc.astype(BF16)
-    for p in (0, FIRST_ORDER):
-        d = place(FIRST_ORDER, p) * 8
-        out_ref[p * 8 : (p + 1) * 8, :] = acc[d : d + 8, :].astype(BF16)
+    for p, d in enumerate(ORDER_GROUP):
+        out_ref[p * 8 : (p + 1) * 8, :] = acc[d * 8 : (d + 1) * 8, :].astype(BF16)
 
 
 def grid_kernel(r_ref, four, sig_hbm, out_hbm, sig, res_v, lhs32, sems):
@@ -164,7 +159,7 @@
         for half in range(2):
             v = [
                 r_ref[p * 8 : (p + 1) * 8, half * 128 : (half + 1) * 128].astype(F32)
-                for p in [place(FIRST_ORDER, g * 8 + t) for t in range(8)]
+                for p in [ORDER_GROUP.index(g * 8 + t) for t in range(8)]
             ]
             for s in (1, 2, 4):
                 first = (block & s) == 0
@@ -221,12 +216,7 @@
         name="vertical",
     )(in_hbm(order_table), in_hbm(degree_table), in_hbm(spectral.reshape(1024, 128)), in_hbm(factors))
     got = lax.all_to_all(
-        send,
-        "level",
-        split_axis=0,
-        concat_axis=0,
-        tiled=True,
-        axis_index_groups=[[place(FIRST_LEVEL, i) for i in range(32)]],
+        send, "level", split_axis=0, concat_axis=0, tiled=True, axis_index_groups=[LEVEL_GROUP]
     )
 
     per, kept = 2, 5
@@ -288,12 +278,7 @@
         name="table",
     )(*[in_hbm(t) for t in tables])
     got2 = lax.all_to_all(
-        fields,
-        "order",
-        split_axis=0,
-        concat_axis=0,
-        tiled=True,
-        axis_index_groups=[[place(FIRST_ORDER, i) for i in range(32)]],
+        fields, "order", split_axis=0, concat_axis=0, tiled=True, axis_index_groups=[ORDER_GROUP]
     )
     return pl.pallas_call(
         grid_kernel,

time: 87.4 us -> 85.7 us (0.981); the launches traced: 86.9 us -> 84.2 us
  waiting for transfers between devices: 15 us -> 11.2 us
  starting transfers between devices: 45.9 us -> 46.9 us
    all_to_all x1, waiting for transfers between devices: 8.6 us -> 6.56 us  [per_device(): lax.all_to_all(send, 'level', split_axis=0, concat_axis=0, tiled=True, ax...]
    all_to_all x1, waiting for transfers between devices: 6.36 us -> 4.61 us  [per_device(): lax.all_to_all(fields, 'order', split_axis=0, concat_axis=0, tiled=True,...]
    all_to_all x1, starting transfers between devices: 8.24 us -> 9.24 us  [per_device(): lax.all_to_all(fields, 'order', split_axis=0, concat_axis=0, tiled=True,...]
where the time goes in v3:
time: 85.7 us; the launch traced here: 84.2 us
  starting transfers between devices  46.9 us (55%)
  Pallas kernels  19.3 us (23%)
  waiting for transfers between devices  11.2 us (13%)
  local copies, waits for them, and re-layouts  3.52 us (4%)
  other arithmetic  3.29 us (4%)
    all_to_all x1, starting transfers between devices, per_device(): lax.all_to_all(send, 'level', split_axis=0, concat_axis=0, tiled=True, ax...  37.6 us
    all_to_all x1, starting transfers between devices, per_device(): lax.all_to_all(fields, 'order', split_axis=0, concat_axis=0, tiled=True,...  9.24 us
    pallas_call x1, Pallas kernels, per_device(): pl.pallas_call(functools.partial(align_kernel, kept), out_shape=(pltpu.VM...  8.06 us
    all_to_all x1, waiting for transfers between devices, per_device(): lax.all_to_all(send, 'level', split_axis=0, concat_axis=0, tiled=True, ax...  6.56 us
    all_to_all x1, waiting for transfers between devices, per_device(): lax.all_to_all(fields, 'order', split_axis=0, concat_axis=0, tiled=True,...  4.61 us
    mul x1, other arithmetic, per_device(): weight * jnp.sin(phase_b)  3.28 us
    pallas_call x1, Pallas kernels, per_device(): pl.pallas_call(table_kernel, out_shape=pltpu.VMEM((3, 2 * waves, points /...  3.08 us
    pallas_call x1, Pallas kernels, per_device(): pl.pallas_call(legendre_kernel, out_shape=pltpu.VMEM((256, 256), BF16), i...  3.02 us
  transfers between devices with their start and end apart: 2, of which 2 were waited for; matrix products, arithmetic and copies ran while one was open for 6% of the time, Pallas kernels for 13%

profile of v3, /device:TPU:1, one launch (start us, length us, event | category | flops | bytes accessed | tf_op | source)
XLA Modules:
  0.0 84.2 jit_solution(14541857776104516073)
XLA Ops:
  0.0 0.0 copy-start.2
  0.0 2.9 %vertical.1 = bf16[512,256]{1,0:T(8,128)(2,1)} custom-call(s32[512]{0:T(512)} %ord_hbm.1, s32[512]{0:T(512)} %deg_hbm.1, bf16[1024,128]{1,0:T(8,128)(2,1)} %bitcast.9, bf16[16,128,128]{2,1,0:T(8,128)(2,1)} %fac_hbm.1), custom_call_target="tpu_custom_call" | custom-call | tf_op jit(solution)/shard_map/vertical/pallas_call | solution.py:200
  2.9 37.6 %all-to-all-start = ((bf16[32,16,256]{2,1,0:T(8,128)(2,1)}), bf16[32,16,256]{2,1,0:T(8,128)(2,1)S(1)}, u32[]{:S(2)}, u32[]{:S(2)}) async-start(bf16[32,16,256]{2,1,0:T(8,128)(2,1)} %bitcast.1), calls=%async_computation | async-start | bytes 524288 | tf_op jit(solution)/shard_map/all_to_all | solution.py:218
  40.5 0.9 %broadcast_in_dim.18 = bf16[8,2,4,1536]{3,2,1,0:T(4,128)(2,1)S(1)} broadcast(bf16[8,4,1536]{2,1,0:T(4,128)(2,1)} %param.9), dimensions={0,2,3} | broadcast | bytes 294912 | tf_op jit(solution)/shard_map/broadcast_in_dim | solution.py:255
  41.5 0.7 reshape.35.sig_hbm
  42.2 0.0 copy-start.1
  42.2 0.7 copy-done.1
  42.9 8.1 %align.1 = (bf16[5,8,256,128]{3,2,1,0:T(8,128)(2,1)S(1)}, bf16[3,8,256,128]{3,2,1,0:T(8,128)(2,1)S(1)}) custom-call(s32[1,512]{1,0:T(1,128)S(1)} %bitcast.8, bf16[16,512,256]{2,1,0:T(8,128)(2,1)} %leg_ref.1), custom_call_target="tpu_custom_call" | custom-call | tf_op jit(solution)/shard_map/align/pallas_call | solution.py:224
  51.0 0.0 copy-start
  51.0 1.1 %copy-done = bf16[3,8,256,128]{3,2,1,0:T(8,128)(2,1)} copy-done((bf16[3,8,256,128]{3,2,1,0:T(8,128)(2,1)}, bf16[3,8,256,128]{3,2,1,0:T(8,128)(2,1)S(1)}, u32[]{:S(2)}) %copy-start) | copy-done | bytes 1572888
  52.1 0.0 copy-done.2
  52.1 3.3 %sine_multiply_fusion = (f32[512,128]{1,0:T(8,128)}, f32[512,128]{1,0:T(8,128)}, f32[512,128]{1,0:T(8,128)}, f32[512,128]{1,0:T(8,128)}) fusion(f32[512]{0:T(512)S(1)} %compare_select_fusion, s32[512]{0:T(512)S(1)} %copy-done.2, s32[128]{0:T(128)S(1)} %and_select_fusion), kind=kLoop, calls=%fused_computation.6 | loop fusion | flops 1310720 | bytes 1053184 | tf_op jit(solution)/shard_map/mul | solution.py:253
  55.4 6.6 %all-to-all-done = bf16[32,16,256]{2,1,0:T(8,128)(2,1)S(1)} async-done(((bf16[32,16,256]{2,1,0:T(8,128)(2,1)}), bf16[32,16,256]{2,1,0:T(8,128)(2,1)S(1)}, u32[]{:S(2)}, u32[]{:S(2)}) %all-to-all-start) | async-done | bytes 262176 | tf_op jit(solution)/shard_map/all_to_all | solution.py:218
  62.0 3.0 %legendre.1 = bf16[256,256]{1,0:T(8,128)(2,1)} custom-call(bf16[5,8,256,128]{3,2,1,0:T(8,128)(2,1)S(1)} %get-tuple-element.22.near_ref, bf16[3,8,256,128]{3,2,1,0:T(8,128)(2,1)} %copy-done, bf16[512,256]{1,0:T(8,128)(2,1)S(1)} %bitcast.6), custom_call_target="tpu_custom_call" | custom-call | tf_op jit(solution)/shard_map/legendre/pallas_call | solution.py:258
  65.0 9.2 %all-to-all-start.1 = ((bf16[32,8,256]{2,1,0:T(8,128)(2,1)}), bf16[32,8,256]{2,1,0:T(8,128)(2,1)S(1)}, u32[]{:S(2)}, u32[]{:S(2)}) async-start(bf16[32,8,256]{2,1,0:T(8,128)(2,1)} %bitcast.4), calls=%async_computation.1 | async-start | bytes 262144 | tf_op jit(solution)/shard_map/all_to_all | solution.py:280
  74.2 3.1 %table.1.four = bf16[3,1024,512]{2,1,0:T(8,128)(2,1)S(1)} custom-call(f32[512,128]{1,0:T(8,128)} %get-tuple-element.30.ca_hbm, f32[512,128]{1,0:T(8,128)} %get-tuple-element.31.sa_hbm, f32[512,128]{1,0:T(8,128)} %get-tuple-element.32.cb_hbm, f32[512,128]{1,0:T(8,128)} %get-tuple-element.33.sb_hbm), custom_call_target="tpu_custom_call" | custom-call | tf_op jit(solution)/shard_map/table/pallas_call | solution.py:271
  77.3 4.6 %all-to-all-done.1 = bf16[32,8,256]{2,1,0:T(8,128)(2,1)S(1)} async-done(((bf16[32,8,256]{2,1,0:T(8,128)(2,1)}), bf16[32,8,256]{2,1,0:T(8,128)(2,1)S(1)}, u32[]{:S(2)}, u32[]{:S(2)}) %all-to-all-start.1) | async-done | bytes 131104 | tf_op jit(solution)/shard_map/all_to_all | solution.py:280
  81.9 2.3 %grid.1 = bf16[8,2,4,1536]{3,2,1,0:T(4,128)(2,1)} custom-call(bf16[256,256]{1,0:T(8,128)(2,1)S(1)} %bitcast.7, bf16[3,1024,512]{2,1,0:T(8,128)(2,1)S(1)} %table.1.four, bf16[64,1536]{1,0:T(8,128)(2,1)} %reshape.35.sig_hbm), custom_call_target="tpu_custom_call" | custom-call | tf_op jit(solution)/shard_map/grid/pallas_call | solution.py:283
  (2 shorter events, 0.0 us)
Async XLA Ops:
  0.0 52.1 %copy-start.2 = (s32[512]{0:T(512)S(1)}, s32[512]{0:T(512)}, u32[]{:S(2)}) copy-start(s32[512]{0:T(512)} %ord_hbm.1) | copy-start | bytes 6148
  2.9 59.1 %all-to-all-start = ((bf16[32,16,256]{2,1,0:T(8,128)(2,1)}), bf16[32,16,256]{2,1,0:T(8,128)(2,1)S(1)}, u32[]{:S(2)}, u32[]{:S(2)}) async-start(bf16[32,16,256]{2,1,0:T(8,128)(2,1)} %bitcast.1), calls=%async_computation | async-start | bytes 524288 | tf_op jit(solution)/shard_map/all_to_all | solution.py:218
  42.2 0.7 copy-start.1
  51.0 1.1 %copy-start = (bf16[3,8,256,128]{3,2,1,0:T(8,128)(2,1)}, bf16[3,8,256,128]{3,2,1,0:T(8,128)(2,1)S(1)}, u32[]{:S(2)}) copy-start(bf16[3,8,256,128]{3,2,1,0:T(8,128)(2,1)S(1)} %get-tuple-element.23.far_hbm) | copy-start | bytes 4718596
  65.0 16.9 %all-to-all-start.1 = ((bf16[32,8,256]{2,1,0:T(8,128)(2,1)}), bf16[32,8,256]{2,1,0:T(8,128)(2,1)S(1)}, u32[]{:S(2)}, u32[]{:S(2)}) async-start(bf16[32,8,256]{2,1,0:T(8,128)(2,1)} %bitcast.4), calls=%async_computation.1 | async-start | bytes 262144 | tf_op jit(solution)/shard_map/all_to_all | solution.py:280

commit v4 on v3

--- a/solution.py
+++ b/solution.py
@@ -15,8 +15,8 @@
     30, 11, 15, 27, 31, 12, 28, 13, 29, 16, 17, 18, 22, 19, 23, 20,
 )
 ORDER_GROUP = (
-    19, 7, 0, 6, 15, 31, 1, 5, 8, 14, 23, 24, 30, 2, 4, 9,
-    13, 16, 22, 25, 29, 3, 10, 12, 17, 21, 26, 28, 11, 18, 20, 27,
+    20, 0, 1, 7, 8, 24, 2, 6, 9, 15, 16, 25, 31, 3, 5, 10,
+    14, 17, 23, 26, 30, 4, 11, 13, 18, 22, 27, 29, 12, 19, 21, 28,
 )
 HBM = pl.BlockSpec(memory_space=pltpu.HBM)
 
@@ -219,7 +219,7 @@
         send, "level", split_axis=0, concat_axis=0, tiled=True, axis_index_groups=[LEVEL_GROUP]
     )
 
-    per, kept = 2, 5
+    per, kept = 2, 6
     groups = 16 // per
     near, far = pl.pallas_call(
         functools.partial(align_kernel, kept),

time: 85.7 us -> 84.7 us (0.988)
  waiting for transfers between devices: 11.2 us -> 9.86 us
  starting transfers between devices: 46.9 us -> 48.1 us
    all_to_all x1, waiting for transfers between devices: 4.61 us -> 3.12 us  [per_device(): lax.all_to_all(fields, 'order', split_axis=0, concat_axis=0, tiled=True,...]
    all_to_all x1, starting transfers between devices: 9.24 us -> 10.5 us  [per_device(): lax.all_to_all(fields, 'order', split_axis=0, concat_axis=0, tiled=True,...]
where the time goes in v4:
time: 84.7 us; the launch traced here: 83.7 us
  starting transfers between devices  48.1 us (57%)
  Pallas kernels  19 us (22%)
  waiting for transfers between devices  9.86 us (12%)
  local copies, waits for them, and re-layouts  3.31 us (4%)
  other arithmetic  3.31 us (4%)
    all_to_all x1, starting transfers between devices, per_device(): lax.all_to_all(send, 'level', split_axis=0, concat_axis=0, tiled=True, ax...  37.6 us
    all_to_all x1, starting transfers between devices, per_device(): lax.all_to_all(fields, 'order', split_axis=0, concat_axis=0, tiled=True,...  10.5 us
    pallas_call x1, Pallas kernels, per_device(): pl.pallas_call(functools.partial(align_kernel, kept), out_shape=(pltpu.VM...  8.06 us
    all_to_all x1, waiting for transfers between devices, per_device(): lax.all_to_all(send, 'level', split_axis=0, concat_axis=0, tiled=True, ax...  6.74 us
    mul x1, other arithmetic, per_device(): weight * jnp.sin(phase_b)  3.3 us
    all_to_all x1, waiting for transfers between devices, per_device(): lax.all_to_all(fields, 'order', split_axis=0, concat_axis=0, tiled=True,...  3.12 us
    pallas_call x1, Pallas kernels, per_device(): pl.pallas_call(table_kernel, out_shape=pltpu.VMEM((3, 2 * waves, points /...  3.08 us
    pallas_call x1, Pallas kernels, per_device(): pl.pallas_call(vertical_kernel, out_shape=pltpu.VMEM((512, 256), BF16), i...  2.87 us
  transfers between devices with their start and end apart: 2, of which 2 were waited for; matrix products, arithmetic and copies ran while one was open for 6% of the time, Pallas kernels for 13%

profile of v4, /device:TPU:1, one launch (start us, length us, event | category | flops | bytes accessed | tf_op | source)
XLA Modules:
  0.0 83.7 jit_solution(17293944668531357202)
XLA Ops:
  0.0 0.0 copy-start.2
  0.0 2.9 %vertical.1 = bf16[512,256]{1,0:T(8,128)(2,1)} custom-call(s32[512]{0:T(512)} %ord_hbm.1, s32[512]{0:T(512)} %deg_hbm.1, bf16[1024,128]{1,0:T(8,128)(2,1)} %bitcast.9, bf16[16,128,128]{2,1,0:T(8,128)(2,1)} %fac_hbm.1), custom_call_target="tpu_custom_call" | custom-call | tf_op jit(solution)/shard_map/vertical/pallas_call | solution.py:200
  2.9 37.6 %all-to-all-start = ((bf16[32,16,256]{2,1,0:T(8,128)(2,1)}), bf16[32,16,256]{2,1,0:T(8,128)(2,1)S(1)}, u32[]{:S(2)}, u32[]{:S(2)}) async-start(bf16[32,16,256]{2,1,0:T(8,128)(2,1)} %bitcast.1), calls=%async_computation | async-start | bytes 524288 | tf_op jit(solution)/shard_map/all_to_all | solution.py:218
  40.5 0.9 %broadcast_in_dim.18 = bf16[8,2,4,1536]{3,2,1,0:T(4,128)(2,1)S(1)} broadcast(bf16[8,4,1536]{2,1,0:T(4,128)(2,1)} %param.9), dimensions={0,2,3} | broadcast | bytes 294912 | tf_op jit(solution)/shard_map/broadcast_in_dim | solution.py:255
  41.5 0.7 reshape.35.sig_hbm
  42.2 0.0 copy-start.1
  42.2 0.7 copy-done.1
  42.9 8.1 %align.1 = (bf16[6,8,256,128]{3,2,1,0:T(8,128)(2,1)S(1)}, bf16[2,8,256,128]{3,2,1,0:T(8,128)(2,1)S(1)}) custom-call(s32[1,512]{1,0:T(1,128)S(1)} %bitcast.8, bf16[16,512,256]{2,1,0:T(8,128)(2,1)} %leg_ref.1), custom_call_target="tpu_custom_call" | custom-call | tf_op jit(solution)/shard_map/align/pallas_call | solution.py:224
  51.0 0.0 copy-start
  51.0 1.0 %copy-done = bf16[2,8,256,128]{3,2,1,0:T(8,128)(2,1)} copy-done((bf16[2,8,256,128]{3,2,1,0:T(8,128)(2,1)}, bf16[2,8,256,128]{3,2,1,0:T(8,128)(2,1)S(1)}, u32[]{:S(2)}) %copy-start) | copy-done | bytes 1048600
  51.9 0.0 copy-done.2
  51.9 3.3 %sine_multiply_fusion = (f32[512,128]{1,0:T(8,128)}, f32[512,128]{1,0:T(8,128)}, f32[512,128]{1,0:T(8,128)}, f32[512,128]{1,0:T(8,128)}) fusion(f32[512]{0:T(512)S(1)} %compare_select_fusion, s32[512]{0:T(512)S(1)} %copy-done.2, s32[128]{0:T(128)S(1)} %and_select_fusion), kind=kLoop, calls=%fused_computation.6 | loop fusion | flops 1310720 | bytes 1053184 | tf_op jit(solution)/shard_map/mul | solution.py:253
  55.2 6.7 %all-to-all-done = bf16[32,16,256]{2,1,0:T(8,128)(2,1)S(1)} async-done(((bf16[32,16,256]{2,1,0:T(8,128)(2,1)}), bf16[32,16,256]{2,1,0:T(8,128)(2,1)S(1)}, u32[]{:S(2)}, u32[]{:S(2)}) %all-to-all-start) | async-done | bytes 262176 | tf_op jit(solution)/shard_map/all_to_all | solution.py:218
  62.0 2.8 %legendre.1 = bf16[256,256]{1,0:T(8,128)(2,1)} custom-call(bf16[6,8,256,128]{3,2,1,0:T(8,128)(2,1)S(1)} %get-tuple-element.22.near_ref, bf16[2,8,256,128]{3,2,1,0:T(8,128)(2,1)} %copy-done, bf16[512,256]{1,0:T(8,128)(2,1)S(1)} %bitcast.6), custom_call_target="tpu_custom_call" | custom-call | tf_op jit(solution)/shard_map/legendre/pallas_call | solution.py:258
  64.8 10.5 %all-to-all-start.1 = ((bf16[32,8,256]{2,1,0:T(8,128)(2,1)}), bf16[32,8,256]{2,1,0:T(8,128)(2,1)S(1)}, u32[]{:S(2)}, u32[]{:S(2)}) async-start(bf16[32,8,256]{2,1,0:T(8,128)(2,1)} %bitcast.4), calls=%async_computation.1 | async-start | bytes 262144 | tf_op jit(solution)/shard_map/all_to_all | solution.py:280
  75.3 3.1 %table.1.four = bf16[3,1024,512]{2,1,0:T(8,128)(2,1)S(1)} custom-call(f32[512,128]{1,0:T(8,128)} %get-tuple-element.30.ca_hbm, f32[512,128]{1,0:T(8,128)} %get-tuple-element.31.sa_hbm, f32[512,128]{1,0:T(8,128)} %get-tuple-element.32.cb_hbm, f32[512,128]{1,0:T(8,128)} %get-tuple-element.33.sb_hbm), custom_call_target="tpu_custom_call" | custom-call | tf_op jit(solution)/shard_map/table/pallas_call | solution.py:271
  78.3 3.1 %all-to-all-done.1 = bf16[32,8,256]{2,1,0:T(8,128)(2,1)S(1)} async-done(((bf16[32,8,256]{2,1,0:T(8,128)(2,1)}), bf16[32,8,256]{2,1,0:T(8,128)(2,1)S(1)}, u32[]{:S(2)}, u32[]{:S(2)}) %all-to-all-start.1) | async-done | bytes 131104 | tf_op jit(solution)/shard_map/all_to_all | solution.py:280
  81.5 2.2 %grid.1 = bf16[8,2,4,1536]{3,2,1,0:T(4,128)(2,1)} custom-call(bf16[256,256]{1,0:T(8,128)(2,1)S(1)} %bitcast.7, bf16[3,1024,512]{2,1,0:T(8,128)(2,1)S(1)} %table.1.four, bf16[64,1536]{1,0:T(8,128)(2,1)} %reshape.35.sig_hbm), custom_call_target="tpu_custom_call" | custom-call | tf_op jit(solution)/shard_map/grid/pallas_call | solution.py:283
  (2 shorter events, 0.0 us)
Async XLA Ops:
  0.0 51.9 %copy-start.2 = (s32[512]{0:T(512)S(1)}, s32[512]{0:T(512)}, u32[]{:S(2)}) copy-start(s32[512]{0:T(512)} %ord_hbm.1) | copy-start | bytes 6148
  2.9 59.1 %all-to-all-start = ((bf16[32,16,256]{2,1,0:T(8,128)(2,1)}), bf16[32,16,256]{2,1,0:T(8,128)(2,1)S(1)}, u32[]{:S(2)}, u32[]{:S(2)}) async-start(bf16[32,16,256]{2,1,0:T(8,128)(2,1)} %bitcast.1), calls=%async_computation | async-start | bytes 524288 | tf_op jit(solution)/shard_map/all_to_all | solution.py:218
  42.2 0.7 copy-start.1
  51.0 1.0 %copy-start = (bf16[2,8,256,128]{3,2,1,0:T(8,128)(2,1)}, bf16[2,8,256,128]{3,2,1,0:T(8,128)(2,1)S(1)}, u32[]{:S(2)}) copy-start(bf16[2,8,256,128]{3,2,1,0:T(8,128)(2,1)S(1)} %get-tuple-element.23.far_hbm) | copy-start | bytes 3145732
  64.8 16.7 %all-to-all-start.1 = ((bf16[32,8,256]{2,1,0:T(8,128)(2,1)}), bf16[32,8,256]{2,1,0:T(8,128)(2,1)S(1)}, u32[]{:S(2)}, u32[]{:S(2)}) async-start(bf16[32,8,256]{2,1,0:T(8,128)(2,1)} %bitcast.4), calls=%async_computation.1 | async-start | bytes 262144 | tf_op jit(solution)/shard_map/all_to_all | solution.py:280
